TPU v7x, 128 devices: a whole 4x4x4 slice. The times are simulated.
128 devices in a mesh: dp: 4 (over z), fsdp: 32 (over y, x, core).
Axes of the slice: x: 4, y: 4, z: 4, core: 2. Of those that a mesh axis runs over, the one named last changes fastest.
Arguments:
- logged: bfloat16 [2048, 8192], P('dp', 'fsdp'), may hold values from -6 to 6
- pairs: int32 [512, 2], P('dp'), may hold values from 0 to 511
- clicks: int32 [512], P('dp'), may hold values 0 or 1
- query_pairs: int32 [32, 2], P('dp'), may hold values from 0 to 511
- query_clicks: int32 [32], P('dp'), may hold values 0 or 1
- first_weight: bfloat16 [8192, 8192], P(None, 'fsdp'), may hold values from -0.0625 to 0.0625
- second_weight: bfloat16 [8192, 8192], P(None, 'fsdp'), may hold values from -0.0625 to 0.0625
- head_weight: float32 [8192], P('fsdp'), may hold values from -0.0625 to 0.0625
Outputs:
- solution: float32 [8192, 8192], P('dp', 'fsdp')
- influence: float32 [512], P('dp')
Inputs may be any that keep to these rules, and one draw needn't show every extreme that they name: Each block of 128 pairs indexes rows within the matching block of 512 logged rows. `query_pairs`: each block of 8 query pairs indexes rows within the matching block of 512 logged rows.
All inputs are finite; a program needn't handle non-finite values. No bound on the sum of `clicks` or of `query_clicks` on one device may be relied on, other than what follows from the above.
Results may differ from a plain program's by a relative error of at most 0.035.
Values may be sent and summed in bfloat16 or wider, within the bound.
A program may use at most 128 MiB of HBM per device.

v0:
```python
import jax
import jax.numpy as jnp
from jax import lax
from jax.sharding import PartitionSpec as P

DAMPING = 0.01


def pair_terms(first_score, second_score, outcome):
    signed = 2.0 * outcome.astype(jnp.float32) - 1.0
    margin = first_score - second_score
    slope_term = -signed * jax.nn.sigmoid(-signed * margin)
    curve_term = jax.nn.sigmoid(signed * margin) * jax.nn.sigmoid(-signed * margin)
    return (slope_term, curve_term)


def solver_total(value):
    return lax.psum(value, ("dp", "fsdp"))


def contract_rows(left, right):
    return lax.dot_general(
        left, right, (((0,), (0,)), ((), ())), preferred_element_type=jnp.float32
    )


def local(
    logged, pairs, clicks, query_pairs, query_clicks, first_weight, second_weight, head_weight
):
    npairs = pairs.shape[0]
    nqueries = query_pairs.shape[0]
    count = 2 * npairs
    row_ids = jnp.concatenate([pairs[:, 0], pairs[:, 1], query_pairs[:, 0], query_pairs[:, 1]])
    local_rows = jnp.take(logged, row_ids, axis=0)
    feats = lax.all_gather(local_rows, "fsdp", axis=1, tiled=True)
    hidden = jnp.tanh(jnp.dot(feats, first_weight, preferred_element_type=jnp.float32)).astype(
        jnp.bfloat16
    )
    second_pre = jnp.dot(
        lax.all_gather(hidden, "fsdp", axis=1, tiled=True),
        second_weight,
        preferred_element_type=jnp.float32,
    )
    output_act = jnp.tanh(second_pre)
    scores_all = lax.psum(jnp.sum(output_act * head_weight, axis=1), "fsdp")
    coef = (head_weight * (1.0 - output_act * output_act)).astype(jnp.bfloat16)
    back_term = lax.dot_general(
        coef, second_weight, (((1,), (1,)), ((), ())), preferred_element_type=jnp.float32
    )
    back = lax.psum_scatter(
        back_term.astype(jnp.bfloat16), "fsdp", scatter_dimension=1, tiled=True
    ).astype(jnp.float32)
    hidden_float = hidden.astype(jnp.float32)
    mixing = (1.0 - hidden_float * hidden_float) * back
    slope_train, curve_train = pair_terms(scores_all[:npairs], scores_all[npairs:count], clicks)
    slope_query = pair_terms(
        scores_all[count : count + nqueries], scores_all[count + nqueries :], query_clicks
    )[0]
    query_err = jnp.concatenate([slope_query, -slope_query])
    query_rows = (query_err[:, None] * mixing[count:]).astype(jnp.bfloat16)
    grad_local = contract_rows(feats[count:], query_rows)
    gradient = lax.psum_scatter(
        grad_local.astype(jnp.bfloat16), "dp", scatter_dimension=0, tiled=True
    ).astype(jnp.float32)
    train_feats = feats[:count]
    train_mix = mixing[:count]

    def apply_curvature(direction):
        packed = direction.astype(jnp.bfloat16)
        gathered = lax.all_gather(packed, "dp", axis=0, tiled=True)
        project = jnp.dot(train_feats, gathered, preferred_element_type=jnp.float32)
        response = lax.psum(jnp.sum(train_mix * project, axis=1), "fsdp")
        rdiff = response[:npairs] - response[npairs:]
        resp_err = jnp.concatenate([curve_train * rdiff, -curve_train * rdiff])
        resp_rows = (resp_err[:, None] * train_mix).astype(jnp.bfloat16)
        term = contract_rows(train_feats, resp_rows)
        return (packed, gathered, term, rdiff)

    norm_first = solver_total(jnp.sum(gradient * gradient))
    packed_first, gathered_first, local_first, rdiff_first = apply_curvature(gradient)
    product_first = lax.psum_scatter(
        local_first.astype(jnp.bfloat16), "dp", scatter_dimension=0, tiled=True
    ).astype(jnp.float32)
    curv_first = (
        solver_total(jnp.sum(packed_first.astype(jnp.float32) * product_first))
        + DAMPING * norm_first
    )
    alpha_first = norm_first / curv_first
    residual_next = gradient - alpha_first * (product_first + DAMPING * gradient)
    norm_next = solver_total(jnp.sum(residual_next * residual_next))
    direction_next = residual_next + norm_next / norm_first * gradient
    packed_next, gathered_next, local_next, rdiff_next = apply_curvature(direction_next)
    damped_part = DAMPING * jnp.sum(direction_next * direction_next)
    product_next = lax.psum_scatter(
        local_next.astype(jnp.bfloat16), "dp", scatter_dimension=0, tiled=True
    ).astype(jnp.float32)
    inner_part = jnp.sum(packed_next.astype(jnp.float32) * product_next) + damped_part
    curv_next = solver_total(inner_part)
    alpha_next = norm_next / curv_next
    solution = alpha_first * gradient + alpha_next * direction_next
    influence = -slope_train * (alpha_first * rdiff_first + alpha_next * rdiff_next)
    return (solution, influence)


def solution(mesh):
    placed = (
        P("dp", "fsdp"),
        P("dp", None),
        P("dp"),
        P("dp", None),
        P("dp"),
        P(None, "fsdp"),
        P(None, "fsdp"),
        P("fsdp"),
    )
    return jax.shard_map(
        local, mesh=mesh, in_specs=placed, out_specs=(P("dp", "fsdp"), P("dp")), check_vma=False
    )
```

profile of v0, /device:TPU:1, one launch (start us, length us, event | category | flops | bytes accessed | tf_op | source)
XLA Modules:
  0.0 815.9 jit_solution(4647815058639752397)
XLA Ops:
  7.2 0.8 slice_bitcast_fusion.3
  8.0 0.8 slice_bitcast_fusion.1
  8.8 2.0 gather_fusion
  10.9 0.8 broadcast_select_fusion
  11.8 53.5 %all-gather.5.cloned.1.call-done = bf16[272,8192]{1,0:T(8,128)(2,1)} async-done(((bf16[272,256]{1,0:T(8,128)(2,1)}), bf16[272,8192]{1,0:T(8,128)(2,1)}) %all-gather.5.cloned.1.call-update) | async-done | bytes 4456464 | tf_op jit(solution)/shard_map/all_gather | solution.py:35
  65.2 5.5 fusion.17
  70.8 49.4 %all-gather.7.cloned.1.call-done = bf16[272,8192]{1,0:T(8,128)(2,1)} async-done(((bf16[272,256]{1,0:T(8,128)(2,1)}), bf16[272,8192]{1,0:T(8,128)(2,1)}) %all-gather.7.cloned.1.call-update) | async-done | bytes 4456464 | tf_op jit(solution)/shard_map/all_gather | solution.py:40
  120.2 5.1 multiply_reduce_fusion.3
  125.4 3.5 convolution_convert_fusion
  128.9 62.7 %psum.49 = f32[272]{0:T(512)S(1)} all-reduce(f32[272]{0:T(512)S(1)} %get-tuple-element.23), channel_id=1, replica_groups=mesh['dp'=4,'fsdp'=32] {'fsdp'}, use_global_device_ids=true, to_apply=%region_1.2 | all-reduce | flops 272 | bytes 2176 | tf_op jit(solution)/shard_map/psum | solution.py:45
  191.7 18.3 %reduce-scatter.5.cloned.1.call-done = bf16[272,256]{1,0:T(8,128)(2,1)} async-done(((bf16[272,8192]{1,0:T(8,128)(2,1)}), bf16[272,256]{1,0:T(8,128)(2,1)}) %reduce-scatter.5.cloned.1.call-update) | async-done | bytes 139280 | tf_op jit(solution)/shard_map/reduce_scatter | solution.py:50
  210.1 1.0 convert_multiply_fusion.5
  211.0 4.2 convolution_convert_fusion.3
  215.3 48.5 %reduce-scatter.7.cloned.1.call-done = bf16[2048,256]{1,0:T(8,128)(2,1)} async-done(((bf16[8192,256]{1,0:T(8,128)(2,1)}), bf16[2048,256]{1,0:T(8,128)(2,1)}) %reduce-scatter.7.cloned.1.call-update) | async-done | bytes 1048592 | tf_op jit(solution)/shard_map/reduce_scatter | solution.py:62
  263.9 49.5 %all-gather.9.cloned.1.call-done = bf16[8192,256]{1,0:T(8,128)(2,1)} async-done(((bf16[2048,256]{1,0:T(8,128)(2,1)}), bf16[8192,256]{1,0:T(8,128)(2,1)}) %all-gather.9.cloned.1.call-update) | async-done | bytes 4194320 | tf_op jit(solution)/shard_map/all_gather | solution.py:70
  313.4 4.8 fusion.22
  318.2 62.7 %psum.51 = f32[256]{0:T(256)S(1)} all-reduce(f32[256]{0:T(256)S(1)} %fusion.22), channel_id=1, replica_groups=mesh['dp'=4,'fsdp'=32] {'fsdp'}, use_global_device_ids=true, to_apply=%region_7.8 | all-reduce | flops 256 | bytes 2048 | tf_op jit(solution)/shard_map/psum | solution.py:72
  380.9 5.5 convolution_convert_fusion.2
  386.5 46.8 %reduce-scatter.9.cloned.1.call-done = bf16[2048,256]{1,0:T(8,128)(2,1)} async-done(((bf16[8192,256]{1,0:T(8,128)(2,1)}), bf16[2048,256]{1,0:T(8,128)(2,1)}) %reduce-scatter.9.cloned.1.call-update) | async-done | bytes 1048592 | tf_op jit(solution)/shard_map/reduce_scatter | solution.py:81
  433.3 2.5 fusion.8
  435.8 64.6 %all-reduce = (f32[]{:T(128)}, f32[]{:T(128)}) all-reduce(f32[]{:T(128)} %get-tuple-element.3, f32[]{:T(128)} %get-tuple-element.2), channel_id=1, replica_groups=mesh['dp'=4,'fsdp'=32] {'dp','fsdp'}, use_global_device_ids=true, to_apply=%region_5.6 | all-reduce | flops 2 | bytes 16 | tf_op jit(solution)/shard_map/psum | solution.py:18
  502.3 2.4 multiply_reduce_fusion.2
  504.7 64.3 %psum.53 = f32[]{:T(128)} all-reduce(f32[]{:T(128)} %multiply_reduce_fusion.2), channel_id=1, replica_groups=mesh['dp'=4,'fsdp'=32] {'dp','fsdp'}, use_global_device_ids=true, to_apply=%region_12.13 | all-reduce | flops 1 | bytes 8 | tf_op jit(solution)/shard_map/psum | solution.py:18
  570.4 2.3 multiply_reduce_fusion
  572.7 45.0 %all-gather.11.cloned.1.call-done = bf16[8192,256]{1,0:T(8,128)(2,1)} async-done(((bf16[2048,256]{1,0:T(8,128)(2,1)}), bf16[8192,256]{1,0:T(8,128)(2,1)}) %all-gather.11.cloned.1.call-update) | async-done | bytes 4194320 | tf_op jit(solution)/shard_map/all_gather | solution.py:70
  617.7 4.8 fusion.19
  622.5 62.7 %psum.54 = f32[256]{0:T(256)S(1)} all-reduce(f32[256]{0:T(256)S(1)} %fusion.19), channel_id=1, replica_groups=mesh['dp'=4,'fsdp'=32] {'fsdp'}, use_global_device_ids=true, to_apply=%region_14.15 | all-reduce | flops 256 | bytes 2048 | tf_op jit(solution)/shard_map/psum | solution.py:72
  685.2 5.5 convolution_convert_fusion.1
  691.5 46.1 %reduce-scatter.11.cloned.1.call-done = bf16[2048,256]{1,0:T(8,128)(2,1)} async-done(((bf16[8192,256]{1,0:T(8,128)(2,1)}), bf16[2048,256]{1,0:T(8,128)(2,1)}) %reduce-scatter.11.cloned.1.call-update) | async-done | bytes 1048592 | tf_op jit(solution)/shard_map/reduce_scatter | solution.py:94
  737.6 2.4 multiply_reduce_fusion.1
  740.6 64.5 %psum.55 = f32[]{:T(128)} all-reduce(f32[]{:T(128)S(6)} %add.83), channel_id=1, replica_groups=mesh['dp'=4,'fsdp'=32] {'dp','fsdp'}, use_global_device_ids=true, to_apply=%region_18.19 | all-reduce | flops 1 | bytes 8 | tf_op jit(solution)/shard_map/psum | solution.py:18
  807.0 2.1 fusion.9
  (45 shorter events, 1.4 us)
Async XLA Ops:
  7.2 1.7 copy-start
  7.2 58.0 %all-gather.5.cloned.1.call-start = ((), (), s32[]{:S(2)}) async-start(), calls=%async_computation.4 | async-start | bytes 4595712 | tf_op jit(solution)/shard_map/all_gather | solution.py:35
  11.7 108.5 %copy-start.6 = (f32[256]{0:T(256)S(1)}, f32[256]{0:T(256)}, u32[]{:S(2)}) copy-start(f32[256]{0:T(256)} %param.15) | copy-start | bytes 3076
  11.7 108.5 %all-gather.7.cloned.1.call-start = ((), (), s32[]{:S(2)}) async-start(), calls=%async_computation.5 | async-start | bytes 4595712 | tf_op jit(solution)/shard_map/all_gather | solution.py:40
  70.8 139.3 %reduce-scatter.5.cloned.1.call-start = ((), (), s32[]{:S(2)}) async-start(), calls=%async_computation.6 | async-start | bytes 4595712 | tf_op jit(solution)/shard_map/reduce_scatter | solution.py:50
  120.2 5.1 copy-start.4
  128.8 62.8 %copy-start.8 = (s32[8]{0:T(128)S(1)}, s32[8]{0:T(128)}, u32[]{:S(2)}) copy-start(s32[8]{0:T(128)} %param.12) | copy-start | bytes 100
  128.8 81.3 %copy-start.5 = (bf16[272,256]{1,0:T(8,128)(2,1)S(1)}, bf16[272,256]{1,0:T(8,128)(2,1)}, u32[]{:S(2)}) copy-start(bf16[272,256]{1,0:T(8,128)(2,1)} %fusion.17) | copy-start | bytes 417796
  128.8 135.0 %reduce-scatter.7.cloned.1.call-start = ((), (), s32[]{:S(2)}) async-start(), calls=%async_computation.7 | async-start | bytes 5242880 | tf_op jit(solution)/shard_map/reduce_scatter | solution.py:62
  215.3 98.1 %all-gather.9.cloned.1.call-start = ((), (), s32[]{:S(2)}) async-start(), calls=%async_computation.8 | async-start | bytes 5242880 | tf_op jit(solution)/shard_map/all_gather | solution.py:70
  263.9 117.0 %copy-start.7 = (s32[128]{0:T(128)S(1)}, s32[128]{0:T(128)}, u32[]{:S(2)}) copy-start(s32[128]{0:T(128)} %param.10) | copy-start | bytes 1540
  263.9 169.4 %reduce-scatter.9.cloned.1.call-start = ((), (), s32[]{:S(2)}) async-start(), calls=%async_computation.9 | async-start | bytes 5242880 | tf_op jit(solution)/shard_map/reduce_scatter | solution.py:81
  386.4 46.9 %copy-start.1 = (bf16[2048,256]{1,0:T(8,128)(2,1)S(1)}, bf16[2048,256]{1,0:T(8,128)(2,1)}, u32[]{:S(2)}) copy-start(bf16[2048,256]{1,0:T(8,128)(2,1)} %reduce-scatter.7.cloned.1.call-done) | copy-start | bytes 3145732
  386.5 231.2 %all-gather.11.cloned.1.call-start = ((), (), s32[]{:S(2)}) async-start(), calls=%async_computation.10 | async-start | bytes 5242880 | tf_op jit(solution)/shard_map/all_gather | solution.py:70
  433.3 137.1 %copy-start.2 = (bf16[2048,256]{1,0:T(8,128)(2,1)S(1)}, bf16[2048,256]{1,0:T(8,128)(2,1)}, u32[]{:S(2)}) copy-start(bf16[2048,256]{1,0:T(8,128)(2,1)} %reduce-scatter.9.cloned.1.call-done) | copy-start | bytes 3145732
  572.7 164.9 %reduce-scatter.11.cloned.1.call-start = ((), (), s32[]{:S(2)}) async-start(), calls=%async_computation.11 | async-start | bytes 5242880 | tf_op jit(solution)/shard_map/reduce_scatter | solution.py:94
  690.7 46.9 %copy-start.3 = (bf16[2048,256]{1,0:T(8,128)(2,1)S(1)}, bf16[2048,256]{1,0:T(8,128)(2,1)}, u32[]{:S(2)}) copy-start(bf16[2048,256]{1,0:T(8,128)(2,1)} %get-tuple-element.12) | copy-start | bytes 3145732
Sparse Core Ops, SparseCore 0:
  11.8 53.3 all-gather.4
  70.9 49.2 all-gather.6
  129.0 81.0 reduce-scatter.4
  215.4 48.3 reduce-scatter.6
  265.4 47.9 all-gather.8
  386.6 46.6 reduce-scatter.8
  572.8 44.8 all-gather.10
  690.9 46.6 reduce-scatter.10
where the time goes:
time: 817 us; the launch traced here: 816 us
  blocking collectives  381 us (47%)
  waiting for transfers between devices  357 us (44%)
  matrix products  38.9 us (5%)
  between operations  20.2 us (2%)
  other arithmetic  14.2 us (2%)
    psum x3, blocking collectives, solver_total(): return lax.psum(value, ('dp', 'fsdp'))  193 us
    psum x2, blocking collectives, apply_curvature(): response = lax.psum(jnp.sum(train_mix * project, axis=1), 'fsdp')  125 us
    all_gather x2, waiting for transfers between devices, apply_curvature(): gathered = lax.all_gather(packed, 'dp', axis=0, tiled=True)  94.4 us
    psum x1, blocking collectives, local(): scores_all = lax.psum(jnp.sum(output_act * head_weight, axis=1), 'fsdp')  62.7 us
    all_gather x1, waiting for transfers between devices, local(): feats = lax.all_gather(local_rows, 'fsdp', axis=1, tiled=True)  53.5 us
    all_gather x1, waiting for transfers between devices, local(): lax.all_gather(hidden, 'fsdp', axis=1, tiled=True)  49.4 us
    reduce_scatter x1, waiting for transfers between devices, local(): lax.psum_scatter(grad_local.astype(jnp.bfloat16), 'dp', scatter_dimension...  48.5 us
    reduce_scatter x1, waiting for transfers between devices, local(): lax.psum_scatter(local_first.astype(jnp.bfloat16), 'dp', scatter_dimensio...  46.8 us
  transfers between devices with their start and end apart: 8, of which 8 were waited for; matrix products, arithmetic and copies ran while one was open for 0% of the time, Pallas kernels for 0%

commit v1 on v0

v1 whole, which is shorter than its diff:
```python
import jax
import jax.numpy as jnp
from jax import lax
from jax.experimental import pallas as pl
from jax.experimental.pallas import tpu as pltpu
from jax.sharding import PartitionSpec as P

DAMPING = 0.01
MESH = pl.DeviceIdType.MESH
F32 = jnp.float32
BF16 = jnp.bfloat16

NP = 128
NT = 256
NQ = 16
ROWS = 272
W = 256


def dot(left, right):
    return jnp.dot(left, right, preferred_element_type=F32)


def dot_nt(left, right):
    return lax.dot_general(left, right, (((1,), (1,)), ((), ())), preferred_element_type=F32)


def kernel(
    logged, pairs, clicks, qpairs, qclicks, w1, w2, head,
    out, infl,
    Fg, Hg, W1o, W1s, W2o, W2s, Ao, As, Ar, Bs, Br, Co, Cs, Pb, RB, Sa, RA, Fz, FT, FU,
    MX, QA, SC, SCr, SP, SPr, SZ, Gf, Gp, Pf, Pp, R0, AR, ARr, ARp, ARpr, ARz,
    loc, wsnd, wrcv, asnd, arcv, bsnd, brcv, csnd, crcv, dsnd, drcv, fsnd, frcv, gsnd, grcv,
    msnd, mrcv, ssnd, srcv, rsnd, rrcv,
):
    z = lax.axis_index("dp")
    f = lax.axis_index("fsdp")
    c = lax.rem(f, 2)
    me = lax.div(f, 2)
    x = lax.rem(me, 4)
    y = lax.div(me, 4)

    def plane(da, db):
        nx = lax.rem(x + da * (1 - c) + db * c + 8, 4)
        ny = lax.rem(y + da * c + db * (1 - c) + 8, 4)
        return ny * 4 + nx

    def dev(da, db):
        return (z, plane(da, db) * 2 + c)

    def zdev(dz):
        return (lax.rem(z + dz + 4, 4), f)

    sibling = (z, me * 2 + 1 - c)
    offsets = [(da, db) for da in range(4) for db in range(4) if (da, db) != (0, 0)]
    partners = [sibling] + [dev(da, db) for da, db in offsets] + [zdev(d) for d in (1, 2, 3)]
    barrier = pltpu.get_barrier_semaphore()
    for partner in partners:
        pl.semaphore_signal(barrier, inc=1, device_id=partner, device_id_type=MESH)
    pl.semaphore_wait(barrier, len(partners))

    sent = []

    def remote(src, dst, send_sem, recv_sem, device):
        return pltpu.make_async_remote_copy(
            src_ref=src, dst_ref=dst, send_sem=send_sem, recv_sem=recv_sem,
            device_id=device, device_id_type=MESH,
        )

    def push(src, dst, send_sem, recv_sem, device):
        copy = remote(src, dst, send_sem, recv_sem, device)
        copy.start()
        sent.append(copy)
        return copy

    w1_own = pltpu.make_async_copy(w1.at[:, c], W1o, loc.at[0])
    w2_own = pltpu.make_async_copy(w2.at[:, c], W2o, loc.at[1])
    w1_own.start()
    w1_sib = push(w1.at[:, 1 - c], W1s, wsnd.at[0], wrcv.at[0], sibling)

    table = logged[...]

    def select(ids):
        lanes = lax.broadcasted_iota(jnp.int32, (ids.shape[0], 512), 1)
        return dot((ids == lanes).astype(F32).astype(BF16), table).astype(BF16)

    Fg[me, 0:NP] = select(pairs[:, 0:1])
    Fg[me, NP:NT] = select(pairs[:, 1:2])
    Fg[me, NT:ROWS] = select(jnp.concatenate([qpairs[:, 0:1], qpairs[:, 1:2]], axis=0))

    def gather_matmul(buf, wo, ws, snd, rcv, ready, acc_o, acc_s):
        first = {}
        for d in (2, 1, 3):
            first[d] = push(buf.at[me], buf.at[me], snd.at[d - 1], rcv.at[d - 1], dev(d, 0))
        for e in (2, 1, 3):
            push(buf.at[me], buf.at[me], snd.at[2 + e], rcv.at[2 + e], dev(0, e))
        ready()
        block = buf[me]
        acc_o[...] = dot(block, wo[me])
        acc_s[...] = dot(block, ws[me])
        for d in (1, 3, 2):
            first[d].wait_recv()
            slot = plane(-d, 0)
            for e in (2, 1, 3):
                push(buf.at[slot], buf.at[slot], snd.at[3 * d + 2 + e], rcv.at[3 * d + 2 + e], dev(0, e))

        @pl.loop(1, 4)
        def _(d):
            slot = plane(-d, 0)
            block = buf[slot]
            acc_o[...] += dot(block, wo[slot])
            acc_s[...] += dot(block, ws[slot])

        @pl.loop(0, 12)
        def _(i):
            slot = plane(-lax.div(i, 3), -(lax.rem(i, 3) + 1))
            remote(buf.at[slot], buf.at[slot], snd.at[3 + i], rcv.at[3 + i], sibling).wait_recv()
            block = buf[slot]
            acc_o[...] += dot(block, wo[slot])
            acc_s[...] += dot(block, ws[slot])

    def w1_ready():
        w2_own.start()
        w1_own.wait()
        w1_sib.wait_recv()

    gather_matmul(Fg, W1o, W1s, asnd, arcv, w1_ready, Ao, As)
    acc_copy = push(As, Ar, dsnd.at[0], drcv.at[0], sibling)
    w2_sib = push(w2.at[:, 1 - c], W2s, wsnd.at[1], wrcv.at[1], sibling)
    acc_copy.wait_recv()
    hidden = jnp.tanh(Ao[...] + Ar[...]).astype(BF16)
    Hg[me] = hidden

    def w2_ready():
        for dz in (1, 2, 3):
            z2 = lax.rem(z + dz, 4)
            fz_copies[dz] = push(
                Fg.at[pl.ds(4 * z2, 4)], Fz.at[z, c], fsnd.at[dz - 1], frcv.at[dz - 1], zdev(dz)
            )
        own = Fg.at[pl.ds(4 * z, 4)]
        fz_own.append(pltpu.make_async_copy(own, Fz.at[z, c], loc.at[2]))
        fz_own[0].start()
        fz_sib.append(push(own, Fz.at[z, c], gsnd.at[0], grcv.at[0], sibling))
        w2_own.wait()
        w2_sib.wait_recv()

    fz_copies, fz_own, fz_sib = {}, [], []
    gather_matmul(Hg, W2o, W2s, bsnd, brcv, w2_ready, Ao, Bs)
    acc_copy = push(Bs, Br, dsnd.at[1], drcv.at[1], sibling)
    acc_copy.wait_recv()
    act = jnp.tanh(Ao[...] + Br[...])
    weights = head[...]
    Co[...] = (weights * (1.0 - act * act)).astype(BF16)
    coef_copy = push(Co, Cs, dsnd.at[2], drcv.at[2], sibling)

    rows128 = lax.broadcasted_iota(jnp.int32, (128, 128), 0)
    lanes128 = lax.broadcasted_iota(jnp.int32, (128, 128), 1)
    eye = rows128 == lanes128

    def to_row(column):
        return jnp.sum(jnp.where(eye, jnp.broadcast_to(column, (128, 128)), 0.0), axis=0, keepdims=True)

    def to_column(row):
        return jnp.sum(jnp.where(eye, jnp.broadcast_to(row, (128, 128)), 0.0), axis=1, keepdims=True)

    part = jnp.sum(act * weights, axis=1, keepdims=True)
    SC[...] = jnp.zeros((8, 128), F32)
    SC[0:1] = to_row(part[0:NP])
    SC[1:2] = to_row(part[NP:NT])
    SC[2:3] = to_row(jnp.concatenate([part[NT:ROWS], jnp.zeros((128 - NQ, 1), F32)], axis=0))
    score_pair = push(SC, SCr, dsnd.at[3], drcv.at[3], sibling)

    coef_copy.wait_recv()

    def back_block(k):
        return dot_nt(Co[...], W2o[k]) + dot_nt(Cs[...], W2s[k])

    order = (2, 1, 3, 0)
    rb = {}
    for da in order:
        for e in (2, 1, 3):
            k = plane(da, e)
            Pb[k] = back_block(k).astype(BF16)
            i = 3 * da + e - 1
            rb[da, e] = push(Pb.at[k], RB.at[i], csnd.at[i], crcv.at[i], dev(0, e))
    score_pair.wait_recv()
    SP[...] = SC[...] + SCr[...]
    sp = [
        push(SP, SPr.at[i], ssnd.at[i], srcv.at[i], dev(da, db)) for i, (da, db) in enumerate(offsets)
    ]
    for da in order:
        Sa[da] = back_block(plane(da, 0))
    ra = {}
    for da in order:
        total = Sa[da]
        for e in (1, 3, 2):
            rb[da, e].wait_recv()
            total += RB[3 * da + e - 1].astype(F32)
        Sa[da] = total
        if da:
            Pb[plane(da, 0)] = total.astype(BF16)
            ra[da] = push(
                Pb.at[plane(da, 0)], RA.at[da - 1], csnd.at[11 + da], crcv.at[11 + da], dev(da, 0)
            )
    score = SP[...]
    for i, copy in enumerate(sp):
        copy.wait_recv()
        score += SPr[i]
    SZ[0] = score
    sz = [push(SZ.at[0], SZ.at[d], ssnd.at[14 + d], srcv.at[14 + d], zdev(d)) for d in (1, 2, 3)]

    for dz in (1, 3, 2):
        fz_copies[dz].wait_recv()
        zs = lax.rem(z - dz + 4, 4)
        fz_sib.append(push(Fz.at[zs, c], Fz.at[zs, c], gsnd.at[dz], grcv.at[dz], sibling))
    fz_own[0].wait()

    def transpose_half(par):
        @pl.loop(0, 4)
        def _(k):
            for zz in range(4):
                FT[par, k, :, zz * NT : (zz + 1) * NT] = Fz[zz, par, k, 0:NT].T
            queries = jnp.concatenate([Fz[zz, par, k, NT:ROWS] for zz in range(4)], axis=0)
            FU[par, k] = queries.astype(F32).T.astype(BF16)

    for copy in fz_sib:
        copy.wait_recv()
    transpose_half(0)
    transpose_half(1)

    total = Sa[0]
    for d in (1, 3, 2):
        ra[d].wait_recv()
        total += RA[d - 1].astype(F32)
    own_hidden = Hg[me].astype(F32)
    mixing = (1.0 - own_hidden * own_hidden) * total

    margin = score[2:3] - pltpu.roll(score[2:3], 120, 1)
    signed = 2.0 * qclicks[...].astype(F32) - 1.0
    slope_query = -signed * jax.nn.sigmoid(-signed * margin[:, 0:8])
    err_row = jnp.concatenate([slope_query, -slope_query, jnp.zeros((1, 112), F32)], axis=1)
    err = to_column(err_row)[0:NQ]
    QA[z] = (err * mixing[NT:ROWS]).astype(BF16)
    qa = [push(QA.at[z], QA.at[z], msnd.at[d - 1], mrcv.at[d - 1], zdev(d)) for d in (1, 2, 3)]
    MX[z] = mixing[0:NT].astype(BF16)
    mx = [push(MX.at[z], MX.at[z], msnd.at[2 + d], mrcv.at[2 + d], zdev(d)) for d in (1, 2, 3)]

    for copy in sz:
        copy.wait_recv()
    train_margin = []
    for zz in range(4):
        tile = SZ[lax.rem(z - zz + 4, 4)]
        train_margin.append(tile[0:1] - tile[1:2])
    margins = jnp.concatenate(train_margin, axis=0)
    curve = jax.nn.sigmoid(margins) * jax.nn.sigmoid(-margins)

    for copy in qa:
        copy.wait_recv()
    squares = jnp.zeros((1, W), F32)
    query_rows = jnp.concatenate([QA[zz] for zz in range(4)], axis=0)
    for par in range(2):
        for k in range(4):
            block = dot(FU[par, k], query_rows)
            squares += jnp.sum(block * block, axis=0, keepdims=True)
            Gf[par, k] = block
            Gp[par, k] = block.astype(BF16)
    for copy in mx:
        copy.wait_recv()

    def responses(direction):
        first, second = [], []
        for zz in range(4):
            project = jnp.zeros((NT, W), F32)
            for par in range(2):
                for k in range(4):
                    project += dot(Fz[zz, par, k, 0:NT], direction[par, k])
            column = jnp.sum(MX[zz].astype(F32) * project, axis=1, keepdims=True)
            first.append(to_row(column[0:NP]))
            second.append(to_row(column[NP:NT]))
        return jnp.concatenate(first + second, axis=0)

    def all_reduce(tile, turn):
        base = turn * 19
        AR[turn] = tile
        pair = push(AR.at[turn], ARr.at[turn], rsnd.at[base], rrcv.at[base], sibling)
        pair.wait_recv()
        tile = AR[turn] + ARr[turn]
        ARp[turn] = tile
        copies = [
            push(ARp.at[turn], ARpr.at[turn, i], rsnd.at[base + 1 + i], rrcv.at[base + 1 + i], dev(da, db))
            for i, (da, db) in enumerate(offsets)
        ]
        for i, copy in enumerate(copies):
            copy.wait_recv()
            tile += ARpr[turn, i]
        ARz[turn, 0] = tile
        copies = [
            push(ARz.at[turn, 0], ARz.at[turn, d], rsnd.at[base + 15 + d], rrcv.at[base + 15 + d], zdev(d))
            for d in (1, 2, 3)
        ]
        for d, copy in enumerate(copies):
            copy.wait_recv()
            tile += ARz[turn, d + 1]
        return tile

    norm_part = jnp.broadcast_to(jnp.sum(squares, axis=1, keepdims=True), (8, 128))
    tile = all_reduce(jnp.concatenate([responses(Gp), norm_part], axis=0), 0)
    rdiff_first = tile[0:4] - tile[4:8]
    norm_first = tile[8:9, 0:1]
    resp_err = curve * rdiff_first
    for zz in range(4):
        scale = to_column(resp_err[zz : zz + 1])
        R0[zz * NT : zz * NT + NP] = (scale * MX[zz, 0:NP].astype(F32)).astype(BF16)
        R0[zz * NT + NP : (zz + 1) * NT] = (-scale * MX[zz, NP:NT].astype(F32)).astype(BF16)
    for par in range(2):
        for k in range(4):
            block = dot(FT[par, k], R0[...])
            Pf[par, k] = block
            Pp[par, k] = block.astype(BF16)
    tile = all_reduce(jnp.concatenate([responses(Pp), norm_part], axis=0), 1)
    rdiff_prod = tile[0:4] - tile[4:8]

    def total_of(value):
        return jnp.sum(jnp.sum(value, axis=1, keepdims=True), axis=0, keepdims=True)

    cross = total_of(curve * rdiff_first * rdiff_first)
    prod_norm = total_of(curve * rdiff_first * rdiff_prod)
    curv_first = cross + DAMPING * norm_first
    alpha_first = norm_first / curv_first
    keep = 1.0 - DAMPING * alpha_first
    norm_next = keep * keep * norm_first - 2.0 * keep * alpha_first * cross + alpha_first * alpha_first * prod_norm
    lead = keep + norm_next / norm_first
    rdiff_next = lead * rdiff_first - alpha_first * rdiff_prod
    direction_norm = lead * lead * norm_first - 2.0 * lead * alpha_first * cross + alpha_first * alpha_first * prod_norm
    curv_next = total_of(curve * rdiff_next * rdiff_next) + DAMPING * direction_norm
    alpha_next = norm_next / curv_next
    on_gradient = alpha_first + alpha_next * lead
    on_product = -alpha_next * alpha_first
    for par in range(2):
        for k in range(4):
            row = (2 * k + par) * W
            out[row : row + W] = on_gradient * Gf[par, k] + on_product * Pf[par, k]

    own_margin = score[0:1] - score[1:2]
    signed = 2.0 * clicks[...].astype(F32) - 1.0
    slope = -signed * jax.nn.sigmoid(-signed * own_margin)
    mine = lax.broadcasted_iota(jnp.int32, (4, 128), 0) == z
    change = alpha_first * rdiff_first + alpha_next * rdiff_next
    infl[...] = -slope * jnp.sum(jnp.where(mine, change, 0.0), axis=0, keepdims=True)

    for copy in sent:
        copy.wait_send()


def local(logged, pairs, clicks, query_pairs, query_clicks, first_weight, second_weight, head_weight):
    vmem = pl.BlockSpec(memory_space=pltpu.VMEM)
    hbm = pl.BlockSpec(memory_space=pl.ANY)
    V = pltpu.VMEM
    dma = pltpu.SemaphoreType.DMA
    block = (ROWS, W)
    scratch = [
        V((16, *block), BF16), V((16, *block), BF16),
        V((16, W, W), BF16), V((16, W, W), BF16), V((16, W, W), BF16), V((16, W, W), BF16),
        V(block, F32), V(block, F32), V(block, F32), V(block, F32), V(block, F32),
        V(block, BF16), V(block, BF16),
        V((16, *block), BF16), V((12, *block), BF16), V((4, *block), F32), V((3, *block), BF16),
        V((4, 2, 4, *block), BF16), V((2, 4, W, 4 * NT), BF16), V((2, 4, W, 4 * NQ), BF16),
        V((4, NT, W), BF16), V((4, NQ, W), BF16),
        V((8, 128), F32), V((8, 128), F32), V((8, 128), F32), V((15, 8, 128), F32), V((4, 8, 128), F32),
        V((2, 4, W, W), F32), V((2, 4, W, W), BF16), V((2, 4, W, W), F32), V((2, 4, W, W), BF16),
        V((4 * NT, W), BF16),
        V((2, 16, 128), F32), V((2, 16, 128), F32), V((2, 16, 128), F32),
        V((2, 15, 16, 128), F32), V((2, 4, 16, 128), F32),
        dma((3,)),
        dma((2,)), dma((2,)), dma((15,)), dma((15,)), dma((15,)), dma((15,)), dma((15,)), dma((15,)),
        dma((4,)), dma((4,)), dma((3,)), dma((3,)), dma((4,)), dma((4,)),
        dma((6,)), dma((6,)), dma((18,)), dma((18,)), dma((38,)), dma((38,)),
    ]
    solved, influence = pl.pallas_call(
        kernel,
        out_shape=(jax.ShapeDtypeStruct((2048, W), F32), jax.ShapeDtypeStruct((1, NP), F32)),
        in_specs=[vmem, vmem, vmem, vmem, vmem, hbm, hbm, vmem],
        out_specs=(vmem, vmem),
        scratch_shapes=scratch,
        compiler_params=pltpu.CompilerParams(
            collective_id=0, has_side_effects=True, vmem_limit_bytes=60 << 20
        ),
    )(
        logged,
        pairs,
        clicks.reshape(1, NP),
        query_pairs,
        query_clicks.reshape(1, 8),
        first_weight.reshape(16, 2, W, W),
        second_weight.reshape(16, 2, W, W),
        head_weight.reshape(1, W),
    )
    return (solved, influence.reshape(NP))


def solution(mesh):
    placed = (
        P("dp", "fsdp"),
        P("dp", None),
        P("dp"),
        P("dp", None),
        P("dp"),
        P(None, "fsdp"),
        P(None, "fsdp"),
        P("fsdp"),
    )
    return jax.shard_map(
        local, mesh=mesh, in_specs=placed, out_specs=(P("dp", "fsdp"), P("dp")), check_vma=False
    )
```

time: 817 us -> 122 us (0.15)
  blocking collectives: 381 us -> 0 us
  waiting for transfers between devices: 357 us -> 0 us
  Pallas kernels: 0 us -> 115 us
  matrix products: 38.9 us -> 0 us
  between operations: 20.2 us -> 0.65 us
  other arithmetic: 14.2 us -> 0 us
    psum x6 -> x0, blocking collectives: 381 us -> none  [the longest x3 193 us: solver_total(): return lax.psum(value, ('dp', 'fsdp'))]
    all_gather x4 -> x0, waiting for transfers between devices: 197 us -> none  [the longest x2 94.4 us: apply_curvature(): gathered = lax.all_gather(packed, 'dp', axis=0, tiled=True)]
    reduce_scatter x4 -> x0, waiting for transfers between devices: 160 us -> none  [the longest x1 48.5 us: local(): lax.psum_scatter(grad_local.astype(jnp.bfloat16), 'dp', scatter_dimension...]
    pallas_call x0 -> x1, Pallas kernels: none -> 115 us  [local(): pl.pallas_call(kernel, out_shape=(jax.ShapeDtypeStruct((2048, W), F32), j...]
    dot_general x8 -> x0, matrix products: 38.9 us -> none  [the longest x3 15.3 us: contract_rows(): lax.dot_general(left, right, (((0,), (0,)), ((), ())), preferred_element_...]
    reduce_sum x4 -> x0, other arithmetic: 9.5 us -> none  [the longest x1 2.46 us: local(): jnp.sum(packed_first.astype(jnp.float32) * product_first)]
  transfers between devices with their start and end apart: 8 -> 0, of which waited for: 8 -> 0; matrix products, arithmetic and copies ran while one was open for 0% -> 0% of each run, Pallas kernels for 0% -> 0%
where the time goes in v1:
time: 122 us
  Pallas kernels  115 us (94%)
  local copies, waits for them, and re-layouts  6.32 us (5%)
    pallas_call x1, Pallas kernels, local(): pl.pallas_call(kernel, out_shape=(jax.ShapeDtypeStruct((2048, W), F32), j...  115 us
    unnamed x6, local copies, waits for them, and re-layouts  6.32 us

profile of v1, /device:TPU:1, one launch (start us, length us, event | category | flops | bytes accessed | tf_op | source)
XLA Modules:
  0.0 121.6 jit_solution(17704947411130308464)
XLA Ops:
  0.6 1.3 %copy.11.qpairs = s32[8,2]{1,0:T(8,128)} copy(s32[8,2]{0,1:T(2,128)} %param.11) | data formatting | bytes 128 | tf_op args[3]
  2.0 1.4 %copy.10.pairs = s32[128,2]{1,0:T(8,128)} copy(s32[128,2]{0,1:T(2,128)} %param.9) | data formatting | bytes 2048 | tf_op args[1]
  3.4 114.6 %shard_map.95 = (f32[2048,256]{1,0:T(8,128)}, f32[1,128]{1,0:T(1,128)}) custom-call(bf16[512,256]{1,0:T(8,128)(2,1)} %logged.1, s32[128,2]{1,0:T(8,128)} %copy.10.pairs, s32[1,128]{1,0:T(1,128)} %bitcast.9, s32[8,2]{1,0:T(8,128)} %copy.11.qpairs, s32[1,8]{1,0:T(1,128)} %bitcast.10, bf16[16,2,256,256]{3,2,1,0:T(8,128)(2,1)} %bitcast.6, ...), custom_call_target="tpu_custom_call" | custom-call | tf_op jit(solution)/shard_map/pallas_call | solution.py:379
  118.0 0.0 copy-start
  118.0 3.0 %copy.14 = f32[2048,256]{1,0:T(8,128)} copy(f32[2048,256]{1,0:T(8,128)} %get-tuple-element.8) | data formatting | bytes 4194304
  121.1 0.0 copy-done
  121.1 0.5 copy.15
Async XLA Ops:
  118.0 3.1 %copy-start = (f32[1,128]{1,0:T(1,128)S(1)}, f32[1,128]{1,0:T(1,128)}, u32[]{:S(2)}) copy-start(f32[1,128]{1,0:T(1,128)} %get-tuple-element.5) | copy-start | bytes 1540

commit v2 on v1

v2 whole, which is shorter than its diff:
```python
import jax
import jax.numpy as jnp
from jax import lax
from jax.experimental import pallas as pl
from jax.experimental.pallas import tpu as pltpu
from jax.sharding import PartitionSpec as P

DAMPING = 0.01
MESH = pl.DeviceIdType.MESH
F32 = jnp.float32
BF16 = jnp.bfloat16

NP = 128
NQ = 16
HALF = (144, 128)
W = 256


def dot(left, right):
    return jnp.dot(left, right, preferred_element_type=F32)


def dot_nt(left, right):
    return lax.dot_general(left, right, (((1,), (1,)), ((), ())), preferred_element_type=F32)


def kernel(
    logged, pairs, clicks, qpairs, qclicks, w1, w2, head,
    g_out, p_out, on_g, on_p, infl,
    F0, F1, H0, H1, W1o, W1s, W2o, W2s,
    Ao0, Ao1, As0, As1, Ar0, Ar1, Bo0, Bo1, Bs0, Bs1, Br0, Br1,
    Co0, Co1, Cs0, Cs1, Pb0, Pb1, RB0, RB1, Sa0, Sa1, RA0, RA1,
    Fz0, Fz1, FT, FU, KT, MX, QA, SC, SCr, SP, SPr, SZ, Gf, Pf, Pp, R0,
    AR, ARr, ARp, ARpr, ARz,
    loc, wsnd, wrcv, asnd, arcv, bsnd, brcv, csnd, crcv, dsnd, drcv, fsnd, frcv, gsnd, grcv,
    ksnd, krcv, msnd, mrcv, ssnd, srcv, rsnd, rrcv,
):
    F, H = (F0, F1), (H0, H1)
    Ao, As, Ar = (Ao0, Ao1), (As0, As1), (Ar0, Ar1)
    Bo, Bs, Br = (Bo0, Bo1), (Bs0, Bs1), (Br0, Br1)
    Co, Cs = (Co0, Co1), (Cs0, Cs1)
    Pb, RB, Sa, RA = (Pb0, Pb1), (RB0, RB1), (Sa0, Sa1), (RA0, RA1)
    Fz = (Fz0, Fz1)

    z = lax.axis_index("dp")
    f = lax.axis_index("fsdp")
    c = lax.rem(f, 2)
    me = lax.div(f, 2)
    x = lax.rem(me, 4)
    y = lax.div(me, 4)

    def plane(da, db):
        nx = lax.rem(x + da * (1 - c) + db * c + 8, 4)
        ny = lax.rem(y + da * c + db * (1 - c) + 8, 4)
        return ny * 4 + nx

    def dev(da, db):
        return (z, plane(da, db) * 2 + c)

    def zdev(dz):
        return (lax.rem(z + dz + 4, 4), f)

    sibling = (z, me * 2 + 1 - c)
    offsets = [(da, db) for da in range(4) for db in range(4) if (da, db) != (0, 0)]
    partners = [sibling] + [dev(da, db) for da, db in offsets] + [zdev(d) for d in (1, 2, 3)]
    barrier = pltpu.get_barrier_semaphore()
    for partner in partners:
        pl.semaphore_signal(barrier, inc=1, device_id=partner, device_id_type=MESH)
    pl.semaphore_wait(barrier, len(partners))

    sent = []

    def remote(src, dst, send_sem, recv_sem, device):
        return pltpu.make_async_remote_copy(
            src_ref=src, dst_ref=dst, send_sem=send_sem, recv_sem=recv_sem,
            device_id=device, device_id_type=MESH,
        )

    def push(src, dst, send_sem, recv_sem, device):
        copy = remote(src, dst, send_sem, recv_sem, device)
        copy.start()
        sent.append(copy)
        return copy

    rows128 = lax.broadcasted_iota(jnp.int32, (128, 128), 0)
    lanes128 = lax.broadcasted_iota(jnp.int32, (128, 128), 1)
    eye = rows128 == lanes128

    def to_row(column):
        return jnp.sum(jnp.where(eye, jnp.broadcast_to(column, (128, 128)), 0.0), axis=0, keepdims=True)

    def to_column(row):
        return jnp.sum(jnp.where(eye, jnp.broadcast_to(row, (128, 128)), 0.0), axis=1, keepdims=True)

    w1_own = pltpu.make_async_copy(w1.at[:, c], W1o, loc.at[0])
    w2_own = pltpu.make_async_copy(w2.at[:, c], W2o, loc.at[1])
    w1_own.start()
    w1_sib = push(w1.at[:, 1 - c], W1s, wsnd.at[0], wrcv.at[0], sibling)

    def gather_send(h, buf, snd, rcv):
        first = {}
        for d in (2, 1, 3):
            first[d] = push(buf[h].at[me], buf[h].at[me], snd.at[h, d - 1], rcv.at[h, d - 1], dev(d, 0))
        for e in (2, 1, 3):
            push(buf[h].at[me], buf[h].at[me], snd.at[h, 2 + e], rcv.at[h, 2 + e], dev(0, e))
        return first

    def gather_forward(h, buf, snd, rcv, first):
        for d in (1, 3, 2):
            first[d].wait_recv()
            slot = plane(-d, 0)
            for e in (2, 1, 3):
                i = 3 * d + 2 + e
                push(buf[h].at[slot], buf[h].at[slot], snd.at[h, i], rcv.at[h, i], dev(0, e))

    def matmul_head(h, buf, wo, ws, acc_o, acc_s):
        block = buf[h][me]
        acc_o[h][...] = dot(block, wo[me])
        acc_s[h][...] = dot(block, ws[me])

        @pl.loop(1, 4)
        def _(d):
            slot = plane(-d, 0)
            block = buf[h][slot]
            acc_o[h][...] += dot(block, wo[slot])
            acc_s[h][...] += dot(block, ws[slot])

    def matmul_tail(h, buf, wo, ws, acc_o, acc_s, snd, rcv):
        @pl.loop(0, 12)
        def _(i):
            slot = plane(-lax.div(i, 3), -(lax.rem(i, 3) + 1))
            remote(buf[h].at[slot], buf[h].at[slot], snd.at[h, 3 + i], rcv.at[h, 3 + i], sibling).wait_recv()
            block = buf[h][slot]
            acc_o[h][...] += dot(block, wo[slot])
            acc_s[h][...] += dot(block, ws[slot])

    def select(row, count):
        lanes = lax.broadcasted_iota(jnp.int32, (128, 512), 1)
        ids = to_column(row.astype(F32)).astype(jnp.int32)
        return dot((ids == lanes).astype(F32).astype(BF16)[0:count], logged[...]).astype(BF16)

    F0[me, 0:NP] = select(pairs[0:1], NP)
    query_ids = jnp.concatenate([qpairs[0:1], qpairs[1:2], jnp.zeros((1, 112), jnp.int32)], axis=1)
    F0[me, NP:144] = select(query_ids, NQ)
    first0 = gather_send(0, F, asnd, arcv)
    F1[me] = select(pairs[1:2], NP)
    first1 = gather_send(1, F, asnd, arcv)
    gather_forward(0, F, asnd, arcv, first0)
    gather_forward(1, F, asnd, arcv, first1)
    w1_own.wait()
    w1_sib.wait_recv()
    w2_own.start()
    w2_sib = push(w2.at[:, 1 - c], W2s, wsnd.at[1], wrcv.at[1], sibling)

    fz_copies, fz_own, fz_sib = {}, {}, []

    def feature_exchange(h):
        for dz in (1, 3, 2):
            z2 = lax.rem(z + dz, 4)
            fz_copies[h, dz] = push(
                F[h].at[pl.ds(4 * z2, 4)], Fz[h].at[z, c], fsnd.at[h, dz - 1], frcv.at[h, dz - 1], zdev(dz)
            )
        own = F[h].at[pl.ds(4 * z, 4)]
        fz_own[h] = pltpu.make_async_copy(own, Fz[h].at[z, c], loc.at[2 + h])
        fz_own[h].start()
        fz_sib.append(push(own, Fz[h].at[z, c], gsnd.at[h, 0], grcv.at[h, 0], sibling))

    def feature_forward(h):
        for dz in (1, 3, 2):
            fz_copies[h, dz].wait_recv()
            zs = lax.rem(z - dz + 4, 4)
            fz_sib.append(push(Fz[h].at[zs, c], Fz[h].at[zs, c], gsnd.at[h, dz], grcv.at[h, dz], sibling))

    matmul_head(0, F, W1o, W1s, Ao, As)
    matmul_tail(0, F, W1o, W1s, Ao, As, asnd, arcv)
    acc0 = push(As0, Ar0, dsnd.at[0], drcv.at[0], sibling)
    feature_exchange(0)
    matmul_head(1, F, W1o, W1s, Ao, As)
    acc0.wait_recv()
    H0[me] = jnp.tanh(Ao0[...] + Ar0[...]).astype(BF16)
    first0 = gather_send(0, H, bsnd, brcv)
    matmul_tail(1, F, W1o, W1s, Ao, As, asnd, arcv)
    acc1 = push(As1, Ar1, dsnd.at[1], drcv.at[1], sibling)
    feature_exchange(1)
    gather_forward(0, H, bsnd, brcv, first0)
    acc1.wait_recv()
    H1[me] = jnp.tanh(Ao1[...] + Ar1[...]).astype(BF16)
    first1 = gather_send(1, H, bsnd, brcv)
    w2_own.wait()
    w2_sib.wait_recv()

    weights = head[...]
    back_copies, coef_copies = {}, {}

    def head_terms(h):
        act = jnp.tanh(Bo[h][...] + Br[h][...])
        Co[h][...] = (weights * (1.0 - act * act)).astype(BF16)
        coef_copies[h] = push(Co[h], Cs[h], dsnd.at[4 + h], drcv.at[4 + h], sibling)
        part = jnp.sum(act * weights, axis=1, keepdims=True)
        SC[h : h + 1] = to_row(part[0:NP])
        if h == 0:
            queries = jnp.concatenate([part[NP:144], jnp.zeros((128 - NQ, 1), F32)], axis=0)
            SC[2:3] = to_row(queries)

    def back_block(h, k):
        return dot_nt(Co[h][...], W2o[k]) + dot_nt(Cs[h][...], W2s[k])

    order = (2, 1, 3, 0)

    def back_send(h):
        coef_copies[h].wait_recv()
        for da in order:
            for e in (2, 1, 3):
                k = plane(da, e)
                Pb[h][k] = back_block(h, k).astype(BF16)
                i = 3 * da + e - 1
                back_copies[h, da, e] = push(
                    Pb[h].at[k], RB[h].at[i], csnd.at[h, i], crcv.at[h, i], dev(0, e)
                )

    def back_own(h):
        for da in order:
            Sa[h][da] = back_block(h, plane(da, 0))

    def back_sum(h):
        for da in order:
            total = Sa[h][da]
            for e in (1, 3, 2):
                back_copies[h, da, e].wait_recv()
                total += RB[h][3 * da + e - 1].astype(F32)
            if da:
                k = plane(da, 0)
                Pb[h][k] = total.astype(BF16)
                back_copies[h, da, 0] = push(
                    Pb[h].at[k], RA[h].at[da - 1], csnd.at[h, 11 + da], crcv.at[h, 11 + da], dev(da, 0)
                )
            else:
                Sa[h][0] = total

    def mixing_of(h):
        total = Sa[h][0]
        for d in (1, 3, 2):
            back_copies[h, d, 0].wait_recv()
            total += RA[h][d - 1].astype(F32)
        own = H[h][me].astype(F32)
        return (1.0 - own * own) * total

    SC[...] = jnp.zeros((8, 128), F32)
    matmul_head(0, H, W2o, W2s, Bo, Bs)
    gather_forward(1, H, bsnd, brcv, first1)
    matmul_tail(0, H, W2o, W2s, Bo, Bs, bsnd, brcv)
    acc0 = push(Bs0, Br0, dsnd.at[2], drcv.at[2], sibling)
    matmul_head(1, H, W2o, W2s, Bo, Bs)
    acc0.wait_recv()
    head_terms(0)
    back_send(0)
    matmul_tail(1, H, W2o, W2s, Bo, Bs, bsnd, brcv)
    acc1 = push(Bs1, Br1, dsnd.at[3], drcv.at[3], sibling)
    back_own(0)
    acc1.wait_recv()
    head_terms(1)
    pair = push(SC, SCr, dsnd.at[6], drcv.at[6], sibling)
    back_send(1)
    pair.wait_recv()
    SP[...] = SC[...] + SCr[...]
    scores = [
        push(SP, SPr.at[i], ssnd.at[i], srcv.at[i], dev(da, db)) for i, (da, db) in enumerate(offsets)
    ]
    feature_forward(0)
    back_sum(0)
    back_own(1)
    feature_forward(1)

    score = SP[...]
    for i, copy in enumerate(scores):
        copy.wait_recv()
        score += SPr[i]
    SZ[0] = score
    sz = [push(SZ.at[0], SZ.at[d], ssnd.at[14 + d], srcv.at[14 + d], zdev(d)) for d in (1, 2, 3)]

    mixing = mixing_of(0)
    margin = score[2:3] - pltpu.roll(score[2:3], 120, 1)
    signed = 2.0 * qclicks[...].astype(F32) - 1.0
    slope_query = -signed * jax.nn.sigmoid(-signed * margin[:, 0:8])
    err_row = jnp.concatenate([slope_query, -slope_query, jnp.zeros((1, 112), F32)], axis=1)
    err = to_column(err_row)[0:NQ]
    QA[z] = (err * mixing[NP:144]).astype(BF16)
    qa = [push(QA.at[z], QA.at[z], msnd.at[d - 1], mrcv.at[d - 1], zdev(d)) for d in (1, 2, 3)]
    MX[0, z] = mixing[0:NP].astype(BF16)
    mx = [push(MX.at[0, z], MX.at[0, z], msnd.at[2 + d], mrcv.at[2 + d], zdev(d)) for d in (1, 2, 3)]

    back_sum(1)
    fz_own[0].wait()
    fz_own[1].wait()
    for copy in fz_sib:
        copy.wait_recv()

    @pl.loop(0, 8)
    def _(b):
        par, k = lax.rem(b, 2), lax.div(b, 2)
        queries = jnp.concatenate([Fz0[zz, par, k, NP:144] for zz in range(4)], axis=0)
        FU[b] = queries.astype(F32).T.astype(BF16)

    kt = []
    for dz in (2, 1, 3, 0):
        zt = lax.rem(z + dz, 4)
        for h in range(2):
            total = jnp.zeros((NP, 4 * NQ), F32)
            for b in range(8):
                total += dot(Fz[h][zt, b % 2, b // 2, 0:NP], FU[b])
            KT[4 + dz, h] = total
        if dz:
            kt.append(push(KT.at[4 + dz], KT.at[dz], ksnd.at[dz - 1], krcv.at[dz - 1], zdev(dz)))

    for copy in qa:
        copy.wait_recv()
    squares = jnp.zeros((1, W), F32)
    query_rows = jnp.concatenate([QA[zz] for zz in range(4)], axis=0)
    for b in range(8):
        block = dot(FU[b], query_rows)
        squares += jnp.sum(block * block, axis=0, keepdims=True)
        Gf[b] = block
    g_copy = pltpu.make_async_copy(Gf, g_out, loc.at[4])
    g_copy.start()
    norm_part = jnp.broadcast_to(jnp.sum(squares, axis=1, keepdims=True), (8, 128))
    cross_rows = KT[4]
    for copy in kt:
        copy.wait_recv()
    for dz in (1, 2, 3):
        cross_rows += KT[dz]
    cross_rows = cross_rows.astype(BF16)

    second = mixing_of(1)
    MX[1, z] = second.astype(BF16)
    mx += [push(MX.at[1, z], MX.at[1, z], msnd.at[5 + d], mrcv.at[5 + d], zdev(d)) for d in (1, 2, 3)]
    own_response = []
    for h, rows in enumerate((mixing[0:NP], second)):
        project = dot(cross_rows[h], query_rows)
        own_response.append(to_row(jnp.sum(rows * project, axis=1, keepdims=True)))
    replica = lax.broadcasted_iota(jnp.int32, (4, 128), 0) == z
    own_tile = jnp.concatenate(
        [jnp.where(replica, jnp.broadcast_to(row, (4, 128)), 0.0) for row in own_response], axis=0
    )

    def all_reduce(tile, turn, between):
        base = turn * 19
        AR[turn] = tile
        pair = push(AR.at[turn], ARr.at[turn], rsnd.at[base], rrcv.at[base], sibling)
        pair.wait_recv()
        tile = AR[turn] + ARr[turn]
        ARp[turn] = tile
        copies = [
            push(ARp.at[turn], ARpr.at[turn, i], rsnd.at[base + 1 + i], rrcv.at[base + 1 + i], dev(da, db))
            for i, (da, db) in enumerate(offsets)
        ]
        between()
        for i, copy in enumerate(copies):
            copy.wait_recv()
            tile += ARpr[turn, i]
        ARz[turn, 0] = tile
        copies = [
            push(ARz.at[turn, 0], ARz.at[turn, d], rsnd.at[base + 15 + d], rrcv.at[base + 15 + d], zdev(d))
            for d in (1, 2, 3)
        ]
        for d, copy in enumerate(copies):
            copy.wait_recv()
            tile += ARz[turn, d + 1]
        return tile

    def transposes():
        @pl.loop(0, 8)
        def _(b):
            par, k = lax.rem(b, 2), lax.div(b, 2)
            for h in range(2):
                for zz in range(4):
                    at = (4 * h + zz) * NP
                    FT[b, :, at : at + NP] = Fz[h][zz, par, k, 0:NP].T

    tile = all_reduce(jnp.concatenate([own_tile, norm_part], axis=0), 0, transposes)

    for copy in sz:
        copy.wait_recv()
    train_margin = []
    for zz in range(4):
        other = SZ[lax.rem(z - zz + 4, 4)]
        train_margin.append(other[0:1] - other[1:2])
    margins = jnp.concatenate(train_margin, axis=0)
    curve = jax.nn.sigmoid(margins) * jax.nn.sigmoid(-margins)
    for copy in mx:
        copy.wait_recv()

    rdiff_first = tile[0:4] - tile[4:8]
    norm_first = tile[8:9, 0:1]
    resp_err = curve * rdiff_first
    for zz in range(4):
        scale = to_column(resp_err[zz : zz + 1])
        R0[zz * NP : (zz + 1) * NP] = (scale * MX[0, zz].astype(F32)).astype(BF16)
        R0[(4 + zz) * NP : (5 + zz) * NP] = (-scale * MX[1, zz].astype(F32)).astype(BF16)
    for b in range(8):
        block = dot(FT[b], R0[...])
        Pf[b] = block
        Pp[b] = block.astype(BF16)
    p_copy = pltpu.make_async_copy(Pf, p_out, loc.at[5])
    p_copy.start()

    response = []
    for h in range(2):
        for zz in range(4):
            project = jnp.zeros((NP, W), F32)
            for b in range(8):
                project += dot(Fz[h][zz, b % 2, b // 2, 0:NP], Pp[b])
            response.append(to_row(jnp.sum(MX[h, zz].astype(F32) * project, axis=1, keepdims=True)))
    tile = all_reduce(jnp.concatenate(response + [norm_part], axis=0), 1, lambda: None)
    rdiff_prod = tile[0:4] - tile[4:8]

    def total_of(value):
        return jnp.sum(jnp.sum(value, axis=1, keepdims=True), axis=0, keepdims=True)

    cross = total_of(curve * rdiff_first * rdiff_first)
    prod_norm = total_of(curve * rdiff_first * rdiff_prod)
    curv_first = cross + DAMPING * norm_first
    alpha_first = norm_first / curv_first
    keep = 1.0 - DAMPING * alpha_first
    norm_next = keep * keep * norm_first - 2.0 * keep * alpha_first * cross + alpha_first * alpha_first * prod_norm
    lead = keep + norm_next / norm_first
    rdiff_next = lead * rdiff_first - alpha_first * rdiff_prod
    direction_norm = lead * lead * norm_first - 2.0 * lead * alpha_first * cross + alpha_first * alpha_first * prod_norm
    curv_next = total_of(curve * rdiff_next * rdiff_next) + DAMPING * direction_norm
    alpha_next = norm_next / curv_next
    on_gradient = alpha_first + alpha_next * lead
    on_product = -alpha_next * alpha_first

    own_margin = score[0:1] - score[1:2]
    signed = 2.0 * clicks[...].astype(F32) - 1.0
    slope = -signed * jax.nn.sigmoid(-signed * own_margin)
    change = alpha_first * rdiff_first + alpha_next * rdiff_next
    on_g[...] = jnp.broadcast_to(on_gradient, (1, W))
    on_p[...] = jnp.broadcast_to(on_product, (1, W))
    infl[...] = -slope * jnp.sum(jnp.where(replica, change, 0.0), axis=0, keepdims=True)

    g_copy.wait()
    p_copy.wait()
    for copy in sent:
        copy.wait_send()


def local(logged, pairs, clicks, query_pairs, query_clicks, first_weight, second_weight, head_weight):
    vmem = pl.BlockSpec(memory_space=pltpu.VMEM)
    hbm = pl.BlockSpec(memory_space=pl.ANY)
    V = pltpu.VMEM
    dma = pltpu.SemaphoreType.DMA

    def halves(dtype, *lead):
        return [V((*lead, rows, W), dtype) for rows in HALF]

    scratch = (
        halves(BF16, 16) + halves(BF16, 16)
        + [V((16, W, W), BF16)] * 4
        + halves(F32) * 6
        + halves(BF16) * 2
        + halves(BF16, 16) + halves(BF16, 12) + halves(F32, 4) + halves(BF16, 3)
        + halves(BF16, 4, 2, 4)
        + [V((8, W, 8 * NP), BF16), V((8, W, 4 * NQ), BF16)]
        + [V((8, 2, NP, 4 * NQ), F32)]
        + [V((2, 4, NP, W), BF16), V((4, NQ, W), BF16)]
        + [V((8, 128), F32)] * 3 + [V((15, 8, 128), F32), V((4, 8, 128), F32)]
        + [V((8, W, W), F32), V((8, W, W), F32), V((8, W, W), BF16)]
        + [V((8 * NP, W), BF16)]
        + [V((2, 16, 128), F32)] * 3 + [V((2, 15, 16, 128), F32), V((2, 4, 16, 128), F32)]
        + [dma((6,))]
        + [dma((2,))] * 2 + [dma((2, 15))] * 6 + [dma((7,))] * 2
        + [dma((2, 3))] * 2 + [dma((2, 4))] * 2 + [dma((3,))] * 2
        + [dma((9,))] * 2 + [dma((18,))] * 2 + [dma((38,))] * 2
    )
    gradient, product, on_gradient, on_product, influence = pl.pallas_call(
        kernel,
        out_shape=(
            jax.ShapeDtypeStruct((8, W, W), F32),
            jax.ShapeDtypeStruct((8, W, W), F32),
            jax.ShapeDtypeStruct((1, W), F32),
            jax.ShapeDtypeStruct((1, W), F32),
            jax.ShapeDtypeStruct((1, NP), F32),
        ),
        in_specs=[vmem, vmem, vmem, vmem, vmem, hbm, hbm, vmem],
        out_specs=(hbm, hbm, vmem, vmem, vmem),
        scratch_shapes=scratch,
        compiler_params=pltpu.CompilerParams(
            collective_id=0, has_side_effects=True, vmem_limit_bytes=60 << 20
        ),
    )(
        logged,
        pairs.T,
        clicks.reshape(1, NP),
        query_pairs.T,
        query_clicks.reshape(1, 8),
        first_weight.reshape(16, 2, W, W),
        second_weight.reshape(16, 2, W, W),
        head_weight.reshape(1, W),
    )
    solved = on_gradient * gradient.reshape(8 * W, W) + on_product * product.reshape(8 * W, W)
    return (solved, influence.reshape(NP))


def solution(mesh):
    placed = (
        P("dp", "fsdp"),
        P("dp", None),
        P("dp"),
        P("dp", None),
        P("dp"),
        P(None, "fsdp"),
        P(None, "fsdp"),
        P("fsdp"),
    )
    return jax.shard_map(
        local, mesh=mesh, in_specs=placed, out_specs=(P("dp", "fsdp"), P("dp")), check_vma=False
    )
```

time: 122 us -> 105 us (0.86)
  Pallas kernels: 115 us -> 100 us
  local copies, waits for them, and re-layouts: 6.32 us -> 0.52 us
  other arithmetic: 0 us -> 3.82 us
    pallas_call x1, Pallas kernels: 115 us -> 100 us  [local(): pl.pallas_call(kernel, out_shape=(jax.ShapeDtypeStruct((8, W, W), F32), j...]
    unnamed x6 -> x3, local copies, waits for them, and re-layouts: 6.32 us -> 0.52 us
    add x0 -> x1, other arithmetic: none -> 3.82 us  [local(): on_gradient * gradient.reshape(8 * W, W)]
where the time goes in v2:
time: 105 us
  Pallas kernels  100 us (95%)
  other arithmetic  3.82 us (4%)
    pallas_call x1, Pallas kernels, local(): pl.pallas_call(kernel, out_shape=(jax.ShapeDtypeStruct((8, W, W), F32), j...  100 us
    add x1, other arithmetic, local(): on_gradient * gradient.reshape(8 * W, W)  3.82 us

profile of v2, /device:TPU:1, one launch (start us, length us, event | category | flops | bytes accessed | tf_op | source)
XLA Modules:
  0.0 105.0 jit_solution(1973963745929352346)
XLA Ops:
  0.6 100.0 %shard_map.95 = (f32[8,256,256]{2,1,0:T(8,128)}, f32[8,256,256]{2,1,0:T(8,128)}, f32[1,256]{1,0:T(1,128)}, f32[1,256]{1,0:T(1,128)}, f32[1,128]{1,0:T(1,128)}) custom-call(bf16[512,256]{1,0:T(8,128)(2,1)} %logged.1, s32[2,128]{1,0:T(2,128)} %bitcast.22, s32[1,128]{1,0:T(1,128)} %bitcast.25, s32[2,8]{1,0:T(2,128)} %bitcast.23, s32[1,8]{1,0:T(1,128)} %bitcast.26, ...), custom_call_target="tpu_custom_call" | custom-call | tf_op jit(solution)/shard_map/pallas_call | solution.py:475
  100.7 0.0 copy-start
  100.7 3.8 %fusion = f32[2048,256]{1,0:T(8,128)} fusion(f32[8,256,256]{2,1,0:T(8,128)} %get-tuple-element.10, f32[8,256,256]{2,1,0:T(8,128)} %get-tuple-element.8, f32[256]{0:T(256)} %bitcast.21, f32[256]{0:T(256)} %bitcast.20), kind=kLoop, calls=%fused_computation.1 | loop fusion | flops 1572864 | bytes 6293504 | tf_op jit(solution)/shard_map/add | solution.py:500
  104.5 0.0 copy-done
  104.5 0.5 copy.11
Async XLA Ops:
  100.7 3.8 %copy-start = (f32[1,128]{1,0:T(1,128)S(1)}, f32[1,128]{1,0:T(1,128)}, u32[]{:S(2)}) copy-start(f32[1,128]{1,0:T(1,128)} %get-tuple-element.11) | copy-start | bytes 1540

commit v3 on v2

--- a/solution.py
+++ b/solution.py
@@ -14,6 +14,8 @@
 NQ = 16
 HALF = (144, 128)
 W = 256
+SPLIT_A = 6
+SPLIT_B = 6
 
 
 def dot(left, right):
@@ -30,7 +32,7 @@
     F0, F1, H0, H1, W1o, W1s, W2o, W2s,
     Ao0, Ao1, As0, As1, Ar0, Ar1, Bo0, Bo1, Bs0, Bs1, Br0, Br1,
     Co0, Co1, Cs0, Cs1, Pb0, Pb1, RB0, RB1, Sa0, Sa1, RA0, RA1,
-    Fz0, Fz1, FT, FU, KT, MX, QA, SC, SCr, SP, SPr, SZ, Gf, Pf, Pp, R0,
+    Fz0, Fz1, FT, FU, KT, MX, QA, SC, SCr, SP, SPr, SZ, Gp, Pp, R0,
     AR, ARr, ARp, ARpr, ARz,
     loc, wsnd, wrcv, asnd, arcv, bsnd, brcv, csnd, crcv, dsnd, drcv, fsnd, frcv, gsnd, grcv,
     ksnd, krcv, msnd, mrcv, ssnd, srcv, rsnd, rrcv,
@@ -101,9 +103,11 @@
         first = {}
         for d in (2, 1, 3):
             first[d] = push(buf[h].at[me], buf[h].at[me], snd.at[h, d - 1], rcv.at[h, d - 1], dev(d, 0))
+        return first
+
+    def gather_across(h, buf, snd, rcv):
         for e in (2, 1, 3):
             push(buf[h].at[me], buf[h].at[me], snd.at[h, 2 + e], rcv.at[h, 2 + e], dev(0, e))
-        return first
 
     def gather_forward(h, buf, snd, rcv, first):
         for d in (1, 3, 2):
@@ -125,8 +129,8 @@
             acc_o[h][...] += dot(block, wo[slot])
             acc_s[h][...] += dot(block, ws[slot])
 
-    def matmul_tail(h, buf, wo, ws, acc_o, acc_s, snd, rcv):
-        @pl.loop(0, 12)
+    def matmul_tail(h, buf, wo, ws, acc_o, acc_s, snd, rcv, start, stop):
+        @pl.loop(start, stop)
         def _(i):
             slot = plane(-lax.div(i, 3), -(lax.rem(i, 3) + 1))
             remote(buf[h].at[slot], buf[h].at[slot], snd.at[h, 3 + i], rcv.at[h, 3 + i], sibling).wait_recv()
@@ -143,10 +147,10 @@
     query_ids = jnp.concatenate([qpairs[0:1], qpairs[1:2], jnp.zeros((1, 112), jnp.int32)], axis=1)
     F0[me, NP:144] = select(query_ids, NQ)
     first0 = gather_send(0, F, asnd, arcv)
+    gather_across(0, F, asnd, arcv)
     F1[me] = select(pairs[1:2], NP)
     first1 = gather_send(1, F, asnd, arcv)
     gather_forward(0, F, asnd, arcv, first0)
-    gather_forward(1, F, asnd, arcv, first1)
     w1_own.wait()
     w1_sib.wait_recv()
     w2_own.start()
@@ -172,17 +176,22 @@
             fz_sib.append(push(Fz[h].at[zs, c], Fz[h].at[zs, c], gsnd.at[h, dz], grcv.at[h, dz], sibling))
 
     matmul_head(0, F, W1o, W1s, Ao, As)
-    matmul_tail(0, F, W1o, W1s, Ao, As, asnd, arcv)
+    matmul_tail(0, F, W1o, W1s, Ao, As, asnd, arcv, 0, SPLIT_A)
+    gather_across(1, F, asnd, arcv)
+    gather_forward(1, F, asnd, arcv, first1)
+    matmul_tail(0, F, W1o, W1s, Ao, As, asnd, arcv, SPLIT_A, 12)
     acc0 = push(As0, Ar0, dsnd.at[0], drcv.at[0], sibling)
     feature_exchange(0)
     matmul_head(1, F, W1o, W1s, Ao, As)
     acc0.wait_recv()
     H0[me] = jnp.tanh(Ao0[...] + Ar0[...]).astype(BF16)
     first0 = gather_send(0, H, bsnd, brcv)
-    matmul_tail(1, F, W1o, W1s, Ao, As, asnd, arcv)
+    gather_across(0, H, bsnd, brcv)
+    matmul_tail(1, F, W1o, W1s, Ao, As, asnd, arcv, 0, SPLIT_B)
+    gather_forward(0, H, bsnd, brcv, first0)
+    matmul_tail(1, F, W1o, W1s, Ao, As, asnd, arcv, SPLIT_B, 12)
     acc1 = push(As1, Ar1, dsnd.at[1], drcv.at[1], sibling)
     feature_exchange(1)
-    gather_forward(0, H, bsnd, brcv, first0)
     acc1.wait_recv()
     H1[me] = jnp.tanh(Ao1[...] + Ar1[...]).astype(BF16)
     first1 = gather_send(1, H, bsnd, brcv)
@@ -247,14 +256,16 @@
 
     SC[...] = jnp.zeros((8, 128), F32)
     matmul_head(0, H, W2o, W2s, Bo, Bs)
+    matmul_tail(0, H, W2o, W2s, Bo, Bs, bsnd, brcv, 0, SPLIT_A)
+    gather_across(1, H, bsnd, brcv)
     gather_forward(1, H, bsnd, brcv, first1)
-    matmul_tail(0, H, W2o, W2s, Bo, Bs, bsnd, brcv)
+    matmul_tail(0, H, W2o, W2s, Bo, Bs, bsnd, brcv, SPLIT_A, 12)
     acc0 = push(Bs0, Br0, dsnd.at[2], drcv.at[2], sibling)
     matmul_head(1, H, W2o, W2s, Bo, Bs)
     acc0.wait_recv()
     head_terms(0)
     back_send(0)
-    matmul_tail(1, H, W2o, W2s, Bo, Bs, bsnd, brcv)
+    matmul_tail(1, H, W2o, W2s, Bo, Bs, bsnd, brcv, 0, 12)
     acc1 = push(Bs1, Br1, dsnd.at[3], drcv.at[3], sibling)
     back_own(0)
     acc1.wait_recv()
@@ -267,9 +278,30 @@
         push(SP, SPr.at[i], ssnd.at[i], srcv.at[i], dev(da, db)) for i, (da, db) in enumerate(offsets)
     ]
     feature_forward(0)
-    back_sum(0)
     back_own(1)
     feature_forward(1)
+    back_sum(0)
+    fz_own[0].wait()
+    fz_own[1].wait()
+    for copy in fz_sib:
+        copy.wait_recv()
+
+    @pl.loop(0, 8)
+    def _(b):
+        par, k = lax.rem(b, 2), lax.div(b, 2)
+        queries = jnp.concatenate([Fz0[zz, par, k, NP:144] for zz in range(4)], axis=0)
+        FU[b] = queries.astype(F32).T.astype(BF16)
+
+    kt = []
+    for dz in (2, 1, 3, 0):
+        zt = lax.rem(z + dz, 4)
+        for h in range(2):
+            total = jnp.zeros((NP, 4 * NQ), F32)
+            for b in range(8):
+                total += dot(Fz[h][zt, b % 2, b // 2, 0:NP], FU[b])
+            KT[4 + dz, h] = total
+        if dz:
+            kt.append(push(KT.at[4 + dz], KT.at[dz], ksnd.at[dz - 1], krcv.at[dz - 1], zdev(dz)))
 
     score = SP[...]
     for i, copy in enumerate(scores):
@@ -290,28 +322,6 @@
     mx = [push(MX.at[0, z], MX.at[0, z], msnd.at[2 + d], mrcv.at[2 + d], zdev(d)) for d in (1, 2, 3)]
 
     back_sum(1)
-    fz_own[0].wait()
-    fz_own[1].wait()
-    for copy in fz_sib:
-        copy.wait_recv()
-
-    @pl.loop(0, 8)
-    def _(b):
-        par, k = lax.rem(b, 2), lax.div(b, 2)
-        queries = jnp.concatenate([Fz0[zz, par, k, NP:144] for zz in range(4)], axis=0)
-        FU[b] = queries.astype(F32).T.astype(BF16)
-
-    kt = []
-    for dz in (2, 1, 3, 0):
-        zt = lax.rem(z + dz, 4)
-        for h in range(2):
-            total = jnp.zeros((NP, 4 * NQ), F32)
-            for b in range(8):
-                total += dot(Fz[h][zt, b % 2, b // 2, 0:NP], FU[b])
-            KT[4 + dz, h] = total
-        if dz:
-            kt.append(push(KT.at[4 + dz], KT.at[dz], ksnd.at[dz - 1], krcv.at[dz - 1], zdev(dz)))
-
     for copy in qa:
         copy.wait_recv()
     squares = jnp.zeros((1, W), F32)
@@ -319,8 +329,8 @@
     for b in range(8):
         block = dot(FU[b], query_rows)
         squares += jnp.sum(block * block, axis=0, keepdims=True)
-        Gf[b] = block
-    g_copy = pltpu.make_async_copy(Gf, g_out, loc.at[4])
+        Gp[b] = block.astype(BF16)
+    g_copy = pltpu.make_async_copy(Gp, g_out, loc.at[4])
     g_copy.start()
     norm_part = jnp.broadcast_to(jnp.sum(squares, axis=1, keepdims=True), (8, 128))
     cross_rows = KT[4]
@@ -398,9 +408,8 @@
         R0[(4 + zz) * NP : (5 + zz) * NP] = (-scale * MX[1, zz].astype(F32)).astype(BF16)
     for b in range(8):
         block = dot(FT[b], R0[...])
-        Pf[b] = block
         Pp[b] = block.astype(BF16)
-    p_copy = pltpu.make_async_copy(Pf, p_out, loc.at[5])
+    p_copy = pltpu.make_async_copy(Pp, p_out, loc.at[5])
     p_copy.start()
 
     response = []
@@ -464,7 +473,7 @@
         + [V((8, 2, NP, 4 * NQ), F32)]
         + [V((2, 4, NP, W), BF16), V((4, NQ, W), BF16)]
         + [V((8, 128), F32)] * 3 + [V((15, 8, 128), F32), V((4, 8, 128), F32)]
-        + [V((8, W, W), F32), V((8, W, W), F32), V((8, W, W), BF16)]
+        + [V((8, W, W), BF16)] * 2
         + [V((8 * NP, W), BF16)]
         + [V((2, 16, 128), F32)] * 3 + [V((2, 15, 16, 128), F32), V((2, 4, 16, 128), F32)]
         + [dma((6,))]
@@ -475,8 +484,8 @@
     gradient, product, on_gradient, on_product, influence = pl.pallas_call(
         kernel,
         out_shape=(
-            jax.ShapeDtypeStruct((8, W, W), F32),
-            jax.ShapeDtypeStruct((8, W, W), F32),
+            jax.ShapeDtypeStruct((8, W, W), BF16),
+            jax.ShapeDtypeStruct((8, W, W), BF16),
             jax.ShapeDtypeStruct((1, W), F32),
             jax.ShapeDtypeStruct((1, W), F32),
             jax.ShapeDtypeStruct((1, NP), F32),
@@ -497,7 +506,7 @@
         second_weight.reshape(16, 2, W, W),
         head_weight.reshape(1, W),
     )
-    solved = on_gradient * gradient.reshape(8 * W, W) + on_product * product.reshape(8 * W, W)
+    solved = on_gradient * gradient.reshape(8 * W, W).astype(F32) + on_product * product.reshape(8 * W, W).astype(F32)
     return (solved, influence.reshape(NP))
 
 

time: 105 us -> 98.4 us (0.937)
  Pallas kernels: 100 us -> 93.9 us
    pallas_call x1, Pallas kernels: 100 us -> 93.9 us  [local(): pl.pallas_call(kernel, out_shape=(jax.ShapeDtypeStruct((8, W, W), BF16),...]
where the time goes in v3:
time: 98.4 us; the launch traced here: 98.2 us
  Pallas kernels  93.9 us (95%)
  other arithmetic  3.21 us (3%)
    pallas_call x1, Pallas kernels, local(): pl.pallas_call(kernel, out_shape=(jax.ShapeDtypeStruct((8, W, W), BF16),...  93.9 us
    add x1, other arithmetic, local(): on_gradient * gradient.reshape(8 * W, W).astype(F32)  3.21 us

profile of v3, /device:TPU:1, one launch (start us, length us, event | category | flops | bytes accessed | tf_op | source)
XLA Modules:
  0.0 98.2 jit_solution(5863726429860224967)
XLA Ops:
  0.6 93.9 %shard_map.95 = (bf16[8,256,256]{2,1,0:T(8,128)(2,1)}, bf16[8,256,256]{2,1,0:T(8,128)(2,1)}, f32[1,256]{1,0:T(1,128)}, f32[1,256]{1,0:T(1,128)}, f32[1,128]{1,0:T(1,128)}) custom-call(bf16[512,256]{1,0:T(8,128)(2,1)} %logged.1, s32[2,128]{1,0:T(2,128)} %bitcast.20, s32[1,128]{1,0:T(1,128)} %bitcast.23, s32[2,8]{1,0:T(2,128)} %bitcast.21, s32[1,8]{1,0:T(1,128)} %bitcast.24, ...), custom_call_target="tpu_custom_call" | custom-call | tf_op jit(solution)/shard_map/pallas_call | solution.py:484
  94.5 0.0 copy-start
  94.5 3.2 %fusion = f32[2048,256]{1,0:T(8,128)} fusion(bf16[8,256,256]{2,1,0:T(8,128)(2,1)} %get-tuple-element.10, bf16[8,256,256]{2,1,0:T(8,128)(2,1)} %get-tuple-element.8, f32[256]{0:T(256)} %bitcast.19, f32[256]{0:T(256)} %bitcast.18), kind=kLoop, calls=%fused_computation.1 | loop fusion | flops 2621440 | bytes 4196352 | tf_op jit(solution)/shard_map/add | solution.py:509
  97.7 0.0 copy-done
  97.7 0.5 copy.11
Async XLA Ops:
  94.5 3.2 %copy-start = (f32[1,128]{1,0:T(1,128)S(1)}, f32[1,128]{1,0:T(1,128)}, u32[]{:S(2)}) copy-start(f32[1,128]{1,0:T(1,128)} %get-tuple-element.11) | copy-start | bytes 1540

commit v4 on v3

--- a/solution.py
+++ b/solution.py
@@ -64,11 +64,10 @@
 
     sibling = (z, me * 2 + 1 - c)
     offsets = [(da, db) for da in range(4) for db in range(4) if (da, db) != (0, 0)]
-    partners = [sibling] + [dev(da, db) for da, db in offsets] + [zdev(d) for d in (1, 2, 3)]
+    partners = [sibling] + [dev(d, 0) for d in (1, 2, 3)] + [dev(0, d) for d in (1, 2, 3)] + [zdev(d) for d in (1, 2, 3)]
     barrier = pltpu.get_barrier_semaphore()
     for partner in partners:
         pl.semaphore_signal(barrier, inc=1, device_id=partner, device_id_type=MESH)
-    pl.semaphore_wait(barrier, len(partners))
 
     sent = []
 
@@ -97,6 +96,17 @@
     w1_own = pltpu.make_async_copy(w1.at[:, c], W1o, loc.at[0])
     w2_own = pltpu.make_async_copy(w2.at[:, c], W2o, loc.at[1])
     w1_own.start()
+
+    def select(row, count):
+        lanes = lax.broadcasted_iota(jnp.int32, (128, 512), 1)
+        ids = to_column(row.astype(F32)).astype(jnp.int32)
+        return dot((ids == lanes).astype(F32).astype(BF16)[0:count], logged[...]).astype(BF16)
+
+    F0[me, 0:NP] = select(pairs[0:1], NP)
+    query_ids = jnp.concatenate([qpairs[0:1], qpairs[1:2], jnp.zeros((1, 112), jnp.int32)], axis=1)
+    F0[me, NP:144] = select(query_ids, NQ)
+    F1[me] = select(pairs[1:2], NP)
+    pl.semaphore_wait(barrier, len(partners))
     w1_sib = push(w1.at[:, 1 - c], W1s, wsnd.at[0], wrcv.at[0], sibling)
 
     def gather_send(h, buf, snd, rcv):
@@ -138,17 +148,8 @@
             acc_o[h][...] += dot(block, wo[slot])
             acc_s[h][...] += dot(block, ws[slot])
 
-    def select(row, count):
-        lanes = lax.broadcasted_iota(jnp.int32, (128, 512), 1)
-        ids = to_column(row.astype(F32)).astype(jnp.int32)
-        return dot((ids == lanes).astype(F32).astype(BF16)[0:count], logged[...]).astype(BF16)
-
-    F0[me, 0:NP] = select(pairs[0:1], NP)
-    query_ids = jnp.concatenate([qpairs[0:1], qpairs[1:2], jnp.zeros((1, 112), jnp.int32)], axis=1)
-    F0[me, NP:144] = select(query_ids, NQ)
     first0 = gather_send(0, F, asnd, arcv)
     gather_across(0, F, asnd, arcv)
-    F1[me] = select(pairs[1:2], NP)
     first1 = gather_send(1, F, asnd, arcv)
     gather_forward(0, F, asnd, arcv, first0)
     w1_own.wait()
@@ -303,6 +304,8 @@
         if dz:
             kt.append(push(KT.at[4 + dz], KT.at[dz], ksnd.at[dz - 1], krcv.at[dz - 1], zdev(dz)))
 
+    back_sum(1)
+
     score = SP[...]
     for i, copy in enumerate(scores):
         copy.wait_recv()
@@ -321,7 +324,6 @@
     MX[0, z] = mixing[0:NP].astype(BF16)
     mx = [push(MX.at[0, z], MX.at[0, z], msnd.at[2 + d], mrcv.at[2 + d], zdev(d)) for d in (1, 2, 3)]
 
-    back_sum(1)
     for copy in qa:
         copy.wait_recv()
     squares = jnp.zeros((1, W), F32)
@@ -406,19 +408,21 @@
         scale = to_column(resp_err[zz : zz + 1])
         R0[zz * NP : (zz + 1) * NP] = (scale * MX[0, zz].astype(F32)).astype(BF16)
         R0[(4 + zz) * NP : (5 + zz) * NP] = (-scale * MX[1, zz].astype(F32)).astype(BF16)
-    for b in range(8):
-        block = dot(FT[b], R0[...])
-        Pp[b] = block.astype(BF16)
+    for b in range(0, 8, 4):
+        rows = FT[b : b + 4].reshape(4 * W, 8 * NP)
+        Pp[b : b + 4] = dot(rows, R0[...]).astype(BF16).reshape(4, W, W)
     p_copy = pltpu.make_async_copy(Pp, p_out, loc.at[5])
     p_copy.start()
 
     response = []
     for h in range(2):
+        project = jnp.zeros((4 * NP, W), F32)
+        for b in range(8):
+            rows = jnp.concatenate([Fz[h][zz, b % 2, b // 2, 0:NP] for zz in range(4)], axis=0)
+            project += dot(rows, Pp[b])
         for zz in range(4):
-            project = jnp.zeros((NP, W), F32)
-            for b in range(8):
-                project += dot(Fz[h][zz, b % 2, b // 2, 0:NP], Pp[b])
-            response.append(to_row(jnp.sum(MX[h, zz].astype(F32) * project, axis=1, keepdims=True)))
+            weighted = MX[h, zz].astype(F32) * project[zz * NP : (zz + 1) * NP]
+            response.append(to_row(jnp.sum(weighted, axis=1, keepdims=True)))
     tile = all_reduce(jnp.concatenate(response + [norm_part], axis=0), 1, lambda: None)
     rdiff_prod = tile[0:4] - tile[4:8]
 

time: 98.4 us -> 97.4 us (0.990)
  Pallas kernels: 93.9 us -> 92.8 us
    pallas_call x1, Pallas kernels: 93.9 us -> 92.8 us  [local(): pl.pallas_call(kernel, out_shape=(jax.ShapeDtypeStruct((8, W, W), BF16),...]
where the time goes in v4:
time: 97.4 us; the launch traced here: 97.2 us
  Pallas kernels  92.8 us (95%)
  other arithmetic  3.21 us (3%)
    pallas_call x1, Pallas kernels, local(): pl.pallas_call(kernel, out_shape=(jax.ShapeDtypeStruct((8, W, W), BF16),...  92.8 us
    add x1, other arithmetic, local(): on_gradient * gradient.reshape(8 * W, W).astype(F32)  3.21 us

profile of v4, /device:TPU:1, one launch (start us, length us, event | category | flops | bytes accessed | tf_op | source)
XLA Modules:
  0.0 97.2 jit_solution(15221235551746622739)
XLA Ops:
  0.6 92.8 %shard_map.95 = (bf16[8,256,256]{2,1,0:T(8,128)(2,1)}, bf16[8,256,256]{2,1,0:T(8,128)(2,1)}, f32[1,256]{1,0:T(1,128)}, f32[1,256]{1,0:T(1,128)}, f32[1,128]{1,0:T(1,128)}) custom-call(bf16[512,256]{1,0:T(8,128)(2,1)} %logged.1, s32[2,128]{1,0:T(2,128)} %bitcast.20, s32[1,128]{1,0:T(1,128)} %bitcast.23, s32[2,8]{1,0:T(2,128)} %bitcast.21, s32[1,8]{1,0:T(1,128)} %bitcast.24, ...), custom_call_target="tpu_custom_call" | custom-call | tf_op jit(solution)/shard_map/pallas_call | solution.py:488
  93.5 0.0 copy-start
  93.5 3.2 %fusion = f32[2048,256]{1,0:T(8,128)} fusion(bf16[8,256,256]{2,1,0:T(8,128)(2,1)} %get-tuple-element.10, bf16[8,256,256]{2,1,0:T(8,128)(2,1)} %get-tuple-element.8, f32[256]{0:T(256)} %bitcast.19, f32[256]{0:T(256)} %bitcast.18), kind=kLoop, calls=%fused_computation.1 | loop fusion | flops 2621440 | bytes 4196352 | tf_op jit(solution)/shard_map/add | solution.py:513
  96.7 0.0 copy-done
  96.7 0.5 copy.11
Async XLA Ops:
  93.5 3.2 %copy-start = (f32[1,128]{1,0:T(1,128)S(1)}, f32[1,128]{1,0:T(1,128)}, u32[]{:S(2)}) copy-start(f32[1,128]{1,0:T(1,128)} %get-tuple-element.11) | copy-start | bytes 1540

commit v5 on v4

--- a/solution.py
+++ b/solution.py
@@ -268,10 +268,10 @@
     back_send(0)
     matmul_tail(1, H, W2o, W2s, Bo, Bs, bsnd, brcv, 0, 12)
     acc1 = push(Bs1, Br1, dsnd.at[3], drcv.at[3], sibling)
-    back_own(0)
     acc1.wait_recv()
     head_terms(1)
     pair = push(SC, SCr, dsnd.at[6], drcv.at[6], sibling)
+    back_own(0)
     back_send(1)
     pair.wait_recv()
     SP[...] = SC[...] + SCr[...]

time: 97.4 us -> 97.4 us (level)
  no operation moved by 1% of the time
where the time goes in v5:
time: 97.4 us; the launch traced here: 97.2 us
  Pallas kernels  92.8 us (95%)
  other arithmetic  3.21 us (3%)
    pallas_call x1, Pallas kernels, local(): pl.pallas_call(kernel, out_shape=(jax.ShapeDtypeStruct((8, W, W), BF16),...  92.8 us
    add x1, other arithmetic, local(): on_gradient * gradient.reshape(8 * W, W).astype(F32)  3.21 us

profile of v5, /device:TPU:1, one launch (start us, length us, event | category | flops | bytes accessed | tf_op | source)
XLA Modules:
  0.0 97.2 jit_solution(8197238710674007207)
XLA Ops:
  0.6 92.8 %shard_map.95 = (bf16[8,256,256]{2,1,0:T(8,128)(2,1)}, bf16[8,256,256]{2,1,0:T(8,128)(2,1)}, f32[1,256]{1,0:T(1,128)}, f32[1,256]{1,0:T(1,128)}, f32[1,128]{1,0:T(1,128)}) custom-call(bf16[512,256]{1,0:T(8,128)(2,1)} %logged.1, s32[2,128]{1,0:T(2,128)} %bitcast.20, s32[1,128]{1,0:T(1,128)} %bitcast.23, s32[2,8]{1,0:T(2,128)} %bitcast.21, s32[1,8]{1,0:T(1,128)} %bitcast.24, ...), custom_call_target="tpu_custom_call" | custom-call | tf_op jit(solution)/shard_map/pallas_call | solution.py:488
  93.5 0.0 copy-start
  93.5 3.2 %fusion = f32[2048,256]{1,0:T(8,128)} fusion(bf16[8,256,256]{2,1,0:T(8,128)(2,1)} %get-tuple-element.10, bf16[8,256,256]{2,1,0:T(8,128)(2,1)} %get-tuple-element.8, f32[256]{0:T(256)} %bitcast.19, f32[256]{0:T(256)} %bitcast.18), kind=kLoop, calls=%fused_computation.1 | loop fusion | flops 2621440 | bytes 4196352 | tf_op jit(solution)/shard_map/add | solution.py:513
  96.7 0.0 copy-done
  96.7 0.5 copy.11
Async XLA Ops:
  93.5 3.2 %copy-start = (f32[1,128]{1,0:T(1,128)S(1)}, f32[1,128]{1,0:T(1,128)}, u32[]{:S(2)}) copy-start(f32[1,128]{1,0:T(1,128)} %get-tuple-element.11) | copy-start | bytes 1540
